TPU v7x, 32 devices: a whole 2x2x4 slice. The times are simulated.
32 devices in a mesh: groups: 2 (over x), rows: 16 (over z, y, core).
Axes of the slice: x: 2, y: 2, z: 4, core: 2. Of those that a mesh axis runs over, the one named last changes fastest.
Arguments:
- row_leaves: int32 [32, 65536], P(None, ('groups', 'rows')), parts along dimension 1, may hold values from 0 to 127
- covariates: bfloat16 [64, 65536], P(None, ('groups', 'rows')), parts along dimension 1, may hold values from -6 to 6
- query_leaves: int32 [32, 128], P(None, 'groups'), parts along dimension 1, may hold values from 0 to 127
- leaf_sizes: int32 [64, 128], P('groups'), parts along dimension 0, may hold values from 128 to 511
Outputs:
- moments: float32 [128, 4096], P(('groups', 'rows')), parts along dimension 0
There are 2 independent parts, one for each index of `groups`. A program takes and returns all parts, laid end to end along the dimension named above; each array names one. Nothing has to cross between parts.
All inputs are finite; a program needn't handle non-finite values.
Results may differ from a plain program's by a relative error of at most 0.0006.
Values may be sent and summed in bfloat16 or wider, within the bound.
A program may use at most 64 MiB of HBM per device.

v0:
```python
import math

import jax
import jax.numpy as jnp
from jax import lax
from jax.sharding import PartitionSpec as P


def moment_rows(covar_block):
    widened = covar_block.astype(jnp.float32)
    width, amount = widened.shape
    product = (widened[:, None, :] * widened[None, :, :]).reshape(width * width, amount)
    return product.astype(jnp.bfloat16)


def query_table(query_leaves, leaf_sizes, amount):
    trees, leaves = leaf_sizes.shape
    inverse = 1.0 / (trees * leaf_sizes.astype(jnp.float32))
    hits = query_leaves.T[:, :, None] == jnp.arange(leaves, dtype=jnp.int32)[None, None, :]
    table = jnp.where(hits, inverse[None, :, :], jnp.float32(0.0)).astype(jnp.bfloat16)
    return table.reshape(amount, trees * leaves)


def kernel_weights(table, leaf_block):
    trees, amount = leaf_block.shape
    leaves = table.shape[1] // trees
    one_hot = (leaf_block[:, None, :] == jnp.arange(leaves, dtype=jnp.int32)[None, :, None]).astype(
        jnp.bfloat16
    )
    one_hot = one_hot.reshape(trees * leaves, amount)
    return jnp.dot(table, one_hot, preferred_element_type=jnp.float32).astype(jnp.bfloat16)


def contract(weights, product):
    return lax.dot_general(
        weights, product, (((1,), (1,)), ((), ())), preferred_element_type=jnp.float32
    )


def per_device(row_leaves, covariates, query_leaves, leaf_sizes):
    width = covariates.shape[0]
    columns = width * width
    local_rows = covariates.shape[1]
    all_queries = query_leaves.shape[1]
    query_dev = all_queries // lax.axis_size("rows")
    row_block = math.gcd(local_rows, 256)
    count_blocks = local_rows // row_block
    table = query_table(query_leaves, leaf_sizes, query_dev * lax.axis_size("rows"))

    def step(position, running):
        first_row = position * row_block
        leaf_block = lax.dynamic_slice_in_dim(row_leaves, first_row, row_block, 1)
        covar_block = lax.dynamic_slice_in_dim(covariates, first_row, row_block, 1)
        weights = kernel_weights(table, leaf_block)
        return running + contract(weights, moment_rows(covar_block))

    return lax.psum_scatter(
        lax.fori_loop(
            0,
            count_blocks,
            step,
            jnp.zeros((query_dev * lax.axis_size("rows"), columns), jnp.float32),
        ),
        "rows",
        scatter_dimension=0,
        tiled=True,
    )


def solution(mesh):
    return jax.shard_map(
        per_device,
        mesh=mesh,
        in_specs=(
            P(None, ("groups", "rows")),
            P(None, ("groups", "rows")),
            P(None, "groups"),
            P("groups", None),
        ),
        out_specs=P(("groups", "rows"), None),
        check_vma=False,
    )
```

profile of v0, /device:TPU:0, one launch (start us, length us, event | category | flops | bytes accessed | tf_op | source)
XLA Modules:
  0.0 189.5 jit_solution(1931076621658625831)
XLA Ops:
  6.5 0.0 all-reduce.3.cloned.1.call-start
  6.5 0.8 copy.6
  7.3 0.7 divide_bitcast_fusion
  8.1 0.0 copy-start
  8.1 76.8 %while.14 = (s32[]{:T(128)}, f32[64,4096]{1,0:T(8,128)}, s32[32,2048]{1,0:T(8,128)}, bf16[64,2048]{1,0:T(8,128)(2,1)}, s32[64,32]{1,0:T(8,128)S(1)}, /*index=5*/...) while((s32[]{:T(128)}, f32[64,4096]{1,0:T(8,128)}, ...), condition=%wide.region_1.2_spmd.clone, body=%wide.region_0.1_spmd.clone.sunk | while | flops 273711104 | bytes 12910765 | solution.py:58
  8.1 0.8 dynamic-slice_convert_fusion.2
  8.9 0.7 multiply_convert_fusion.2
  9.6 0.8 constant_dynamic-slice_fusion.3
  10.3 1.7 fusion.18
  12.0 0.3 eq.114
  12.4 5.1 %convolution_add_fusion.2 = f32[64,4096]{1,0:T(8,128)} fusion(bf16[4096,256]{1,0:T(8,128)(2,1)S(1)} %bitcast.36, bf16[4096,256]{1,0:T(8,128)(2,1)} %fusion.18, f32[64,4096]{1,0:T(8,128)} %get-tuple-element.198, s32[8,8,32,128]{3,2,1,0:T(8,128)S(1)} %bitcast.37, bf16[4096]{0:T(1024)(128)(2,1)S(1)} %get-tuple-element.214, ...), kind=kOutput, calls=%fused_computation.1.clone.1 | convolution fusion | flops 269500416 | bytes 7364609 | tf_op jit(solution)/shard_map/while/body/eval_jaxpr/dot_general | solution.py:35
  17.5 0.8 dynamic-slice_convert_fusion.2
  18.2 0.7 multiply_convert_fusion.2
  18.9 0.8 constant_dynamic-slice_fusion.3
  19.7 1.7 fusion.18
  21.4 0.3 eq.114
  21.7 5.4 %convolution_add_fusion.2 = f32[64,4096]{1,0:T(8,128)} fusion(bf16[4096,256]{1,0:T(8,128)(2,1)S(1)} %bitcast.36, bf16[4096,256]{1,0:T(8,128)(2,1)} %fusion.18, f32[64,4096]{1,0:T(8,128)} %get-tuple-element.198, s32[8,8,32,128]{3,2,1,0:T(8,128)S(1)} %bitcast.37, bf16[4096]{0:T(1024)(128)(2,1)S(1)} %get-tuple-element.214, ...), kind=kOutput, calls=%fused_computation.1.clone.1 | convolution fusion | flops 269500416 | bytes 7364609 | tf_op jit(solution)/shard_map/while/body/eval_jaxpr/dot_general | solution.py:35
  27.1 0.8 dynamic-slice_convert_fusion.2
  27.8 0.7 multiply_convert_fusion.2
  28.5 0.8 constant_dynamic-slice_fusion.3
  29.3 1.7 fusion.18
  31.0 0.3 eq.114
  31.4 5.4 %convolution_add_fusion.2 = f32[64,4096]{1,0:T(8,128)} fusion(bf16[4096,256]{1,0:T(8,128)(2,1)S(1)} %bitcast.36, bf16[4096,256]{1,0:T(8,128)(2,1)} %fusion.18, f32[64,4096]{1,0:T(8,128)} %get-tuple-element.198, s32[8,8,32,128]{3,2,1,0:T(8,128)S(1)} %bitcast.37, bf16[4096]{0:T(1024)(128)(2,1)S(1)} %get-tuple-element.214, ...), kind=kOutput, calls=%fused_computation.1.clone.1 | convolution fusion | flops 269500416 | bytes 7364609 | tf_op jit(solution)/shard_map/while/body/eval_jaxpr/dot_general | solution.py:35
  36.7 0.8 dynamic-slice_convert_fusion.2
  37.5 0.7 multiply_convert_fusion.2
  38.2 0.8 constant_dynamic-slice_fusion.3
  38.9 1.7 fusion.18
  40.6 0.3 eq.114
  41.0 5.4 %convolution_add_fusion.2 = f32[64,4096]{1,0:T(8,128)} fusion(bf16[4096,256]{1,0:T(8,128)(2,1)S(1)} %bitcast.36, bf16[4096,256]{1,0:T(8,128)(2,1)} %fusion.18, f32[64,4096]{1,0:T(8,128)} %get-tuple-element.198, s32[8,8,32,128]{3,2,1,0:T(8,128)S(1)} %bitcast.37, bf16[4096]{0:T(1024)(128)(2,1)S(1)} %get-tuple-element.214, ...), kind=kOutput, calls=%fused_computation.1.clone.1 | convolution fusion | flops 269500416 | bytes 7364609 | tf_op jit(solution)/shard_map/while/body/eval_jaxpr/dot_general | solution.py:35
  46.3 0.8 dynamic-slice_convert_fusion.2
  47.1 0.7 multiply_convert_fusion.2
  47.8 0.8 constant_dynamic-slice_fusion.3
  48.6 1.7 fusion.18
  50.3 0.3 eq.114
  50.6 5.4 %convolution_add_fusion.2 = f32[64,4096]{1,0:T(8,128)} fusion(bf16[4096,256]{1,0:T(8,128)(2,1)S(1)} %bitcast.36, bf16[4096,256]{1,0:T(8,128)(2,1)} %fusion.18, f32[64,4096]{1,0:T(8,128)} %get-tuple-element.198, s32[8,8,32,128]{3,2,1,0:T(8,128)S(1)} %bitcast.37, bf16[4096]{0:T(1024)(128)(2,1)S(1)} %get-tuple-element.214, ...), kind=kOutput, calls=%fused_computation.1.clone.1 | convolution fusion | flops 269500416 | bytes 7364609 | tf_op jit(solution)/shard_map/while/body/eval_jaxpr/dot_general | solution.py:35
  56.0 0.8 dynamic-slice_convert_fusion.2
  56.7 0.7 multiply_convert_fusion.2
  57.4 0.8 constant_dynamic-slice_fusion.3
  58.2 1.7 fusion.18
  59.9 0.3 eq.114
  60.2 5.4 %convolution_add_fusion.2 = f32[64,4096]{1,0:T(8,128)} fusion(bf16[4096,256]{1,0:T(8,128)(2,1)S(1)} %bitcast.36, bf16[4096,256]{1,0:T(8,128)(2,1)} %fusion.18, f32[64,4096]{1,0:T(8,128)} %get-tuple-element.198, s32[8,8,32,128]{3,2,1,0:T(8,128)S(1)} %bitcast.37, bf16[4096]{0:T(1024)(128)(2,1)S(1)} %get-tuple-element.214, ...), kind=kOutput, calls=%fused_computation.1.clone.1 | convolution fusion | flops 269500416 | bytes 7364609 | tf_op jit(solution)/shard_map/while/body/eval_jaxpr/dot_general | solution.py:35
  65.6 0.8 dynamic-slice_convert_fusion.2
  66.3 0.7 multiply_convert_fusion.2
  67.0 0.8 constant_dynamic-slice_fusion.3
  67.8 1.7 fusion.18
  69.5 0.3 eq.114
  69.9 5.4 %convolution_add_fusion.2 = f32[64,4096]{1,0:T(8,128)} fusion(bf16[4096,256]{1,0:T(8,128)(2,1)S(1)} %bitcast.36, bf16[4096,256]{1,0:T(8,128)(2,1)} %fusion.18, f32[64,4096]{1,0:T(8,128)} %get-tuple-element.198, s32[8,8,32,128]{3,2,1,0:T(8,128)S(1)} %bitcast.37, bf16[4096]{0:T(1024)(128)(2,1)S(1)} %get-tuple-element.214, ...), kind=kOutput, calls=%fused_computation.1.clone.1 | convolution fusion | flops 269500416 | bytes 7364609 | tf_op jit(solution)/shard_map/while/body/eval_jaxpr/dot_general | solution.py:35
  75.2 0.8 dynamic-slice_convert_fusion.2
  76.0 0.7 multiply_convert_fusion.2
  76.7 0.8 constant_dynamic-slice_fusion.3
  77.4 1.7 fusion.18
  79.1 0.3 eq.114
  79.5 5.4 %convolution_add_fusion.2 = f32[64,4096]{1,0:T(8,128)} fusion(bf16[4096,256]{1,0:T(8,128)(2,1)S(1)} %bitcast.36, bf16[4096,256]{1,0:T(8,128)(2,1)} %fusion.18, f32[64,4096]{1,0:T(8,128)} %get-tuple-element.198, s32[8,8,32,128]{3,2,1,0:T(8,128)S(1)} %bitcast.37, bf16[4096]{0:T(1024)(128)(2,1)S(1)} %get-tuple-element.214, ...), kind=kOutput, calls=%fused_computation.1.clone.1 | convolution fusion | flops 269500416 | bytes 7364609 | tf_op jit(solution)/shard_map/while/body/eval_jaxpr/dot_general | solution.py:35
  84.8 0.0 all-reduce.3.cloned.1.call-update
  84.9 0.0 copy-done
  84.9 0.6 dynamic-slice
  86.1 95.0 %all-reduce.3.cloned.1.call-done = f32[64,4096]{1,0:T(8,128)} async-done(((f32[64,4096]{1,0:T(8,128)}), f32[64,4096]{1,0:T(8,128)}) %all-reduce.3.cloned.1.call-update) | async-done | bytes 1048592
  181.1 1.5 constant_dynamic-slice_fusion.1
  (10 shorter events, 0.0 us)
Async XLA Ops:
  6.5 174.6 %all-reduce.3.cloned.1.call-start = ((), (), s32[]{:S(2)}) async-start(), calls=%async_computation | async-start | bytes 2097152
  8.1 76.8 %copy-start = (u32[32]{0:T(128)S(1)}, u32[32]{0:T(128)}, u32[]{:S(2)}) copy-start(u32[32]{0:T(128)} %constant.39) | copy-start | bytes 388
Sparse Core Ops, SparseCore 0:
  85.0 96.0 all-reduce.2
where the time goes:
time: 191 us; the launch traced here: 189 us
  waiting for transfers between devices  95 us (50%)
  matrix products  42.6 us (22%)
  other arithmetic  26 us (14%)
  between operations  14.1 us (7%)
  local copies, waits for them, and re-layouts  11.7 us (6%)
    unnamed x2, waiting for transfers between devices  95 us
    dot_general x8, matrix products, contract(): lax.dot_general(weights, product, (((1,), (1,)), ((), ())), preferred_ele...  42.6 us
    while x8, other arithmetic  13.7 us
    dynamic_slice x8, local copies, waits for them, and re-layouts, step(): leaf_block = lax.dynamic_slice_in_dim(row_leaves, first_row, row_block, 1)  6.14 us
    convert_element_type x8, other arithmetic, moment_rows(): widened = covar_block.astype(jnp.float32)  6.11 us
    convert_element_type x8, other arithmetic, moment_rows(): return product.astype(jnp.bfloat16)  5.45 us
  transfers between devices with their start and end apart: 1, of which 1 were waited for; matrix products, arithmetic and copies ran while one was open for 0% of the time, Pallas kernels for 0%

commit v1 on v0

v1 whole, which is shorter than its diff:
```python
import functools

import jax
import jax.numpy as jnp
from jax import lax
from jax.experimental import pallas as pl
from jax.experimental.pallas import tpu as pltpu
from jax.sharding import PartitionSpec as P

CHUNKS = 4
GROUP = 4
LANES = 128


def kernel(n, rl_ref, x_ref, ql_ref, ls_ref, o_ref, xf, qb, wb, w_s, prod, part, s2, s3, r1, r2, r3,
           ss1, rs1, ss2, rs2, ss3, rs3):
    trees, rows = rl_ref.shape
    width = x_ref.shape[0]
    queries = ql_ref.shape[1]
    t = queries // n
    nz = n // 4
    sub = nz * t
    cols = width * width // CHUNKS
    me = lax.axis_index("rows")
    core = lax.rem(me, 2)
    y = lax.rem(me // 2, 2)
    z = me // 4

    sibling = me + 1 - 2 * core
    ypeer = me + 2 - 4 * y
    zpeers = [lax.rem(me + 4 * d, n) for d in range(1, nz)]
    barrier = pltpu.get_barrier_semaphore()
    for peer in [sibling, ypeer] + zpeers:
        pl.semaphore_signal(barrier, inc=1, device_id={"rows": peer}, device_id_type=pl.DeviceIdType.MESH)

    xf[...] = x_ref[...].astype(jnp.float32)

    inverse = 1.0 / (trees * ls_ref[...].astype(jnp.float32))
    ql = ql_ref[...]
    leaf_cols, weight_cols = [], []
    for first in range(0, queries, LANES):
        piece = ql[:, first:first + LANES]
        if piece.shape[1] < LANES:
            piece = jnp.concatenate([piece] * (LANES // piece.shape[1]), axis=1)
        chosen = jnp.take_along_axis(inverse, piece, axis=1).astype(jnp.bfloat16).astype(jnp.float32)
        leaf_cols.append(piece.T)
        weight_cols.append(chosen.T)

    def ordered(cols_list):
        out = []
        for c in range(2):
            for b in range(2):
                for k in range(nz):
                    first = (k * 4 + b * 2 + c) * t
                    out.append(cols_list[first // LANES][first % LANES:first % LANES + t])
        return jnp.concatenate(out, axis=0)

    leaf_t = ordered(leaf_cols)
    weight_t = ordered(weight_cols)
    for b in range(trees):
        qb[b] = jnp.broadcast_to(leaf_t[:, b:b + 1], (queries, LANES))
        wb[b] = jnp.broadcast_to(weight_t[:, b:b + 1], (queries, LANES))

    tile = 64
    halves = 2
    def weights_step(step, carry):
        at = step // (queries // tile) * (halves * LANES)
        q0 = lax.rem(step, queries // tile) * tile
        at = pl.multiple_of(at, halves * LANES)
        q0 = pl.multiple_of(q0, tile)
        accs = [jnp.zeros((tile, LANES), jnp.float32) for _ in range(halves)]
        for b in range(trees):
            leaf = qb[b, pl.ds(q0, tile), :]
            weight = wb[b, pl.ds(q0, tile), :]
            for h in range(halves):
                row = rl_ref[b:b + 1, pl.ds(pl.multiple_of(at + h * LANES, LANES), LANES)]
                accs[h] = accs[h] + jnp.where(leaf == row, weight, 0.0)
        w_s[pl.ds(q0, tile), pl.ds(at, halves * LANES)] = jnp.concatenate(accs, axis=1).astype(jnp.bfloat16)
        return carry

    lax.fori_loop(0, (rows // (halves * LANES)) * (queries // tile), weights_step, 0)

    per_chunk = width // CHUNKS // GROUP

    def compute(c):
        def body(g, carry):
            for jj in range(GROUP):
                j = (c * per_chunk + g) * GROUP + jj
                xb = jnp.broadcast_to(xf[pl.ds(j, 1), :], (16, rows)).astype(jnp.bfloat16)
                for k in range(0, width, 16):
                    prod[jj * width + k:jj * width + k + 16, :] = x_ref[k:k + 16, :] * xb
            res = lax.dot_general(w_s[...], prod[...], (((1,), (1,)), ((), ())),
                                  preferred_element_type=jnp.float32)
            off = pl.multiple_of(g * GROUP * width, GROUP * width)
            for a in range(2):
                for b in range(2):
                    part[c, a, b, :, pl.ds(off, GROUP * width)] = res[(a * 2 + b) * sub:(a * 2 + b + 1) * sub, :]
            return carry
        lax.fori_loop(0, per_chunk, body, 0)

    def copy(src, dst, ssem, rsem, peer):
        return pltpu.make_async_remote_copy(src_ref=src, dst_ref=dst, send_sem=ssem, recv_sem=rsem,
                                            device_id={"rows": peer}, device_id_type=pl.DeviceIdType.MESH)

    def c1(c):
        return copy(part.at[c, 1 - core], r1.at[c], ss1.at[c], rs1.at[c], sibling)

    def c2(c):
        return copy(s2.at[c], r2.at[c], ss2.at[c], rs2.at[c], ypeer)

    def c3(c, d):
        return copy(s3.at[c, lax.rem(z + d, nz)], r3.at[c, d - 1], ss3.at[c, d - 1], rs3.at[c, d - 1], zpeers[d - 1])

    def stage2(c):
        c1(c).wait_recv()
        s2[c] = part[c, core, 1 - y] + r1[c, 1 - y]
        c2(c).start()

    def stage3(c):
        c2(c).wait_recv()
        total = part[c, core, y] + r1[c, y] + r2[c]
        for k in range(nz):
            s3[c, k] = total[k * t:(k + 1) * t, :]
        for d in range(1, nz):
            c3(c, d).start()

    def finish(c):
        total = s3[c, z]
        for d in range(1, nz):
            c3(c, d).wait_recv()
            total = total + r3[c, d - 1]
        o_ref[:, c * cols:(c + 1) * cols] = total

    for s in range(CHUNKS + 3):
        if s < CHUNKS:
            compute(s)
            if s == 0:
                pl.semaphore_wait(barrier, 1 + nz)
            c1(s).start()
        if 0 <= s - 1 < CHUNKS:
            stage2(s - 1)
        if 0 <= s - 2 < CHUNKS:
            stage3(s - 2)
        if 0 <= s - 3 < CHUNKS:
            finish(s - 3)
    for c in range(CHUNKS):
        c1(c).wait_send()
        c2(c).wait_send()
        for d in range(1, nz):
            c3(c, d).wait_send()


def per_device(row_leaves, covariates, query_leaves, leaf_sizes):
    n = lax.axis_size("rows")
    trees, rows = row_leaves.shape
    width = covariates.shape[0]
    queries = query_leaves.shape[1]
    t = queries // n
    nz = n // 4
    sub = nz * t
    cols = width * width // CHUNKS
    vmem = pl.BlockSpec(memory_space=pltpu.VMEM)
    f32 = jnp.float32
    dma = pltpu.SemaphoreType.DMA
    return pl.pallas_call(
        functools.partial(kernel, n),
        out_shape=jax.ShapeDtypeStruct((t, width * width), f32),
        in_specs=[vmem] * 4,
        out_specs=vmem,
        scratch_shapes=[
            pltpu.VMEM((width, rows), f32),
            pltpu.VMEM((trees, queries, LANES), jnp.int32),
            pltpu.VMEM((trees, queries, LANES), f32),
            pltpu.VMEM((queries, rows), jnp.bfloat16),
            pltpu.VMEM((GROUP * width, rows), jnp.bfloat16),
            pltpu.VMEM((CHUNKS, 2, 2, sub, cols), f32),
            pltpu.VMEM((CHUNKS, sub, cols), f32),
            pltpu.VMEM((CHUNKS, nz, t, cols), f32),
            pltpu.VMEM((CHUNKS, 2, sub, cols), f32),
            pltpu.VMEM((CHUNKS, sub, cols), f32),
            pltpu.VMEM((CHUNKS, nz - 1, t, cols), f32),
            dma((CHUNKS,)), dma((CHUNKS,)), dma((CHUNKS,)), dma((CHUNKS,)),
            dma((CHUNKS, nz - 1)), dma((CHUNKS, nz - 1)),
        ],
        compiler_params=pltpu.CompilerParams(collective_id=0, has_side_effects=True,
                                             vmem_limit_bytes=56 << 20),
    )(row_leaves, covariates, query_leaves, leaf_sizes)


def solution(mesh):
    return jax.shard_map(
        per_device,
        mesh=mesh,
        in_specs=(
            P(None, ("groups", "rows")),
            P(None, ("groups", "rows")),
            P(None, "groups"),
            P("groups", None),
        ),
        out_specs=P(("groups", "rows"), None),
        check_vma=False,
    )
```

time: 191 us -> 27 us (0.14)
  waiting for transfers between devices: 95 us -> 0 us
  matrix products: 42.6 us -> 0 us
  other arithmetic: 26 us -> 0 us
  Pallas kernels: 0 us -> 25.4 us
  between operations: 14.1 us -> 0.01 us
  local copies, waits for them, and re-layouts: 11.7 us -> 1.47 us
    unnamed x2 -> x0, waiting for transfers between devices: 95 us -> none
    dot_general x8 -> x0, matrix products: 42.6 us -> none  [contract(): lax.dot_general(weights, product, (((1,), (1,)), ((), ())), preferred_ele...]
    pallas_call x0 -> x1, Pallas kernels: none -> 25.4 us  [per_device(): pl.pallas_call(functools.partial(kernel, n), out_shape=jax.ShapeDtypeStru...]
    while x8 -> x0, other arithmetic: 13.7 us -> none
    convert_element_type x16 -> x0, other arithmetic: 11.6 us -> none  [the longest x8 6.11 us: moment_rows(): widened = covar_block.astype(jnp.float32)]
    dynamic_slice x8 -> x0, local copies, waits for them, and re-layouts: 6.14 us -> none  [step(): leaf_block = lax.dynamic_slice_in_dim(row_leaves, first_row, row_block, 1)]
    eq x17 -> x0, local copies, waits for them, and re-layouts: 2.66 us -> none  [the longest x9 2.64 us: query_table(): query_leaves.T[:, :, None]]
  transfers between devices with their start and end apart: 1 -> 0, of which waited for: 1 -> 0; matrix products, arithmetic and copies ran while one was open for 0% -> 0% of each run, Pallas kernels for 0% -> 0%
where the time goes in v1:
time: 27 us; the launch traced here: 26.8 us
  Pallas kernels  25.4 us (94%)
  local copies, waits for them, and re-layouts  1.47 us (5%)
    pallas_call x1, Pallas kernels, per_device(): pl.pallas_call(functools.partial(kernel, n), out_shape=jax.ShapeDtypeStru...  25.4 us
    unnamed x1, local copies, waits for them, and re-layouts  1.47 us

profile of v1, /device:TPU:0, one launch (start us, length us, event | category | flops | bytes accessed | tf_op | source)
XLA Modules:
  0.0 26.8 jit_solution(13529971940934185540)
XLA Ops:
  0.0 25.4 %shard_map.46 = f32[4,4096]{1,0:T(4,128)} custom-call(s32[32,2048]{1,0:T(8,128)} %rl_ref.1, bf16[64,2048]{1,0:T(8,128)(2,1)} %x_ref.1, s32[32,64]{1,0:T(8,128)} %ql_ref.1, s32[32,128]{1,0:T(8,128)} %ls_ref.1), custom_call_target="tpu_custom_call" | custom-call | tf_op jit(solution)/shard_map/pallas_call | solution.py:165
  25.4 1.5 %copy.6 = f32[4,4096]{1,0:T(4,128)} copy(f32[4,4096]{1,0:T(4,128)} %shard_map.46) | data formatting | bytes 131072

commit v2 on v1

--- a/solution.py
+++ b/solution.py
@@ -9,28 +9,40 @@
 
 CHUNKS = 4
 GROUP = 4
+EARLY = 2
 LANES = 128
 
 
-def kernel(n, rl_ref, x_ref, ql_ref, ls_ref, o_ref, xf, qb, wb, w_s, prod, part, s2, s3, r1, r2, r3,
-           ss1, rs1, ss2, rs2, ss3, rs3):
+def coded(value):
+    largest = jnp.maximum(jnp.max(jnp.abs(value), axis=1, keepdims=True), 1e-30)
+    power = jnp.floor(256.0 * jnp.log2(32000.0 / largest))
+    whole = jnp.round(value * jnp.exp2(power * (1.0 / 256.0))).astype(jnp.int32)
+    tail = jnp.broadcast_to(power.astype(jnp.int32), (value.shape[0], LANES))
+    return jnp.concatenate([whole, tail], axis=1)
+
+
+def decoded(code):
+    wide = code.astype(jnp.int32).astype(jnp.float32)
+    cols = wide.shape[1] - LANES
+    return wide[:, :cols] * jnp.exp2(wide[:, cols:cols + 1] * (-1.0 / 256.0))
+
+
+def kernel(n, rl_ref, x_ref, ql_ref, ls_ref, o_ref, xf, qb, wb, w_s, prod, part, own, s3, r1, r3,
+           ss1, rs1, ss3, rs3):
     trees, rows = rl_ref.shape
     width = x_ref.shape[0]
     queries = ql_ref.shape[1]
     t = queries // n
-    nz = n // 4
+    nz = n // 2
     sub = nz * t
     cols = width * width // CHUNKS
     me = lax.axis_index("rows")
     core = lax.rem(me, 2)
-    y = lax.rem(me // 2, 2)
-    z = me // 4
-
+    z = me // 2
     sibling = me + 1 - 2 * core
-    ypeer = me + 2 - 4 * y
-    zpeers = [lax.rem(me + 4 * d, n) for d in range(1, nz)]
+    zpeers = [lax.rem(me + 2 * d, n) for d in range(1, nz)]
     barrier = pltpu.get_barrier_semaphore()
-    for peer in [sibling, ypeer] + zpeers:
+    for peer in [sibling] + zpeers:
         pl.semaphore_signal(barrier, inc=1, device_id={"rows": peer}, device_id_type=pl.DeviceIdType.MESH)
 
     xf[...] = x_ref[...].astype(jnp.float32)
@@ -49,10 +61,9 @@
     def ordered(cols_list):
         out = []
         for c in range(2):
-            for b in range(2):
-                for k in range(nz):
-                    first = (k * 4 + b * 2 + c) * t
-                    out.append(cols_list[first // LANES][first % LANES:first % LANES + t])
+            for k in range(nz):
+                first = (k * 2 + c) * t
+                out.append(cols_list[first // LANES][first % LANES:first % LANES + t])
         return jnp.concatenate(out, axis=0)
 
     leaf_t = ordered(leaf_cols)
@@ -93,8 +104,7 @@
                                   preferred_element_type=jnp.float32)
             off = pl.multiple_of(g * GROUP * width, GROUP * width)
             for a in range(2):
-                for b in range(2):
-                    part[c, a, b, :, pl.ds(off, GROUP * width)] = res[(a * 2 + b) * sub:(a * 2 + b + 1) * sub, :]
+                part[c, a, :, pl.ds(off, GROUP * width)] = res[a * sub:(a + 1) * sub, :]
             return carry
         lax.fori_loop(0, per_chunk, body, 0)
 
@@ -105,47 +115,41 @@
     def c1(c):
         return copy(part.at[c, 1 - core], r1.at[c], ss1.at[c], rs1.at[c], sibling)
 
-    def c2(c):
-        return copy(s2.at[c], r2.at[c], ss2.at[c], rs2.at[c], ypeer)
-
     def c3(c, d):
         return copy(s3.at[c, lax.rem(z + d, nz)], r3.at[c, d - 1], ss3.at[c, d - 1], rs3.at[c, d - 1], zpeers[d - 1])
 
-    def stage2(c):
+    def exchange(c):
         c1(c).wait_recv()
-        s2[c] = part[c, core, 1 - y] + r1[c, 1 - y]
-        c2(c).start()
-
-    def stage3(c):
-        c2(c).wait_recv()
-        total = part[c, core, y] + r1[c, y] + r2[c]
+        total = part[c, core] + r1[c]
+        code = coded(total)
         for k in range(nz):
-            s3[c, k] = total[k * t:(k + 1) * t, :]
+            own[c, k] = total[k * t:(k + 1) * t, :]
+            s3[c, k] = code[k * t:(k + 1) * t, :].astype(jnp.int16)
         for d in range(1, nz):
             c3(c, d).start()
 
     def finish(c):
-        total = s3[c, z]
+        total = own[c, z]
         for d in range(1, nz):
             c3(c, d).wait_recv()
-            total = total + r3[c, d - 1]
+            total = total + decoded(r3[c, d - 1])
         o_ref[:, c * cols:(c + 1) * cols] = total
 
-    for s in range(CHUNKS + 3):
-        if s < CHUNKS:
-            compute(s)
-            if s == 0:
-                pl.semaphore_wait(barrier, 1 + nz)
-            c1(s).start()
-        if 0 <= s - 1 < CHUNKS:
-            stage2(s - 1)
-        if 0 <= s - 2 < CHUNKS:
-            stage3(s - 2)
-        if 0 <= s - 3 < CHUNKS:
-            finish(s - 3)
+    for c in range(CHUNKS):
+        compute(c)
+        if c == EARLY - 1:
+            pl.semaphore_wait(barrier, nz)
+            for e in range(EARLY):
+                c1(e).start()
+        if c >= EARLY:
+            c1(c).start()
+            for e in (range(EARLY) if c == EARLY else [c - 1]):
+                exchange(e)
+    exchange(CHUNKS - 1)
+    for c in range(CHUNKS):
+        finish(c)
     for c in range(CHUNKS):
         c1(c).wait_send()
-        c2(c).wait_send()
         for d in range(1, nz):
             c3(c, d).wait_send()
 
@@ -156,7 +160,7 @@
     width = covariates.shape[0]
     queries = query_leaves.shape[1]
     t = queries // n
-    nz = n // 4
+    nz = n // 2
     sub = nz * t
     cols = width * width // CHUNKS
     vmem = pl.BlockSpec(memory_space=pltpu.VMEM)
@@ -173,13 +177,12 @@
             pltpu.VMEM((trees, queries, LANES), f32),
             pltpu.VMEM((queries, rows), jnp.bfloat16),
             pltpu.VMEM((GROUP * width, rows), jnp.bfloat16),
-            pltpu.VMEM((CHUNKS, 2, 2, sub, cols), f32),
+            pltpu.VMEM((CHUNKS, 2, sub, cols), f32),
+            pltpu.VMEM((CHUNKS, nz, t, cols), f32),
+            pltpu.VMEM((CHUNKS, nz, t, cols + LANES), jnp.int16),
             pltpu.VMEM((CHUNKS, sub, cols), f32),
-            pltpu.VMEM((CHUNKS, nz, t, cols), f32),
-            pltpu.VMEM((CHUNKS, 2, sub, cols), f32),
-            pltpu.VMEM((CHUNKS, sub, cols), f32),
-            pltpu.VMEM((CHUNKS, nz - 1, t, cols), f32),
-            dma((CHUNKS,)), dma((CHUNKS,)), dma((CHUNKS,)), dma((CHUNKS,)),
+            pltpu.VMEM((CHUNKS, nz - 1, t, cols + LANES), jnp.int16),
+            dma((CHUNKS,)), dma((CHUNKS,)),
             dma((CHUNKS, nz - 1)), dma((CHUNKS, nz - 1)),
         ],
         compiler_params=pltpu.CompilerParams(collective_id=0, has_side_effects=True,

time: 27 us -> 24.8 us (0.919)
  Pallas kernels: 25.4 us -> 23.1 us
    pallas_call x1, Pallas kernels: 25.4 us -> 23.1 us  [per_device(): pl.pallas_call(functools.partial(kernel, n), out_shape=jax.ShapeDtypeStru...]
where the time goes in v2:
time: 24.8 us; the launch traced here: 24.6 us
  Pallas kernels  23.1 us (93%)
  local copies, waits for them, and re-layouts  1.47 us (6%)
    pallas_call x1, Pallas kernels, per_device(): pl.pallas_call(functools.partial(kernel, n), out_shape=jax.ShapeDtypeStru...  23.1 us
    unnamed x1, local copies, waits for them, and re-layouts  1.47 us

profile of v2, /device:TPU:0, one launch (start us, length us, event | category | flops | bytes accessed | tf_op | source)
XLA Modules:
  0.0 24.6 jit_solution(14152715393121916749)
XLA Ops:
  0.0 23.1 %shard_map.46 = f32[4,4096]{1,0:T(4,128)} custom-call(s32[32,2048]{1,0:T(8,128)} %rl_ref.1, bf16[64,2048]{1,0:T(8,128)(2,1)} %x_ref.1, s32[32,64]{1,0:T(8,128)} %ql_ref.1, s32[32,128]{1,0:T(8,128)} %ls_ref.1), custom_call_target="tpu_custom_call" | custom-call | tf_op jit(solution)/shard_map/pallas_call | solution.py:169
  23.1 1.5 %copy.6 = f32[4,4096]{1,0:T(4,128)} copy(f32[4,4096]{1,0:T(4,128)} %shard_map.46) | data formatting | bytes 131072

commit v3 on v2

--- a/solution.py
+++ b/solution.py
@@ -7,10 +7,15 @@
 from jax.experimental.pallas import tpu as pltpu
 from jax.sharding import PartitionSpec as P
 
-CHUNKS = 4
-GROUP = 4
-EARLY = 2
+CHUNKS = 2
+SIDE = 16
+EARLY = 1
 LANES = 128
+
+
+def blocks_of(width):
+    count = width // SIDE
+    return [(a, b) for a in range(count) for b in range(a, count)]
 
 
 def coded(value):
@@ -27,7 +32,7 @@
     return wide[:, :cols] * jnp.exp2(wide[:, cols:cols + 1] * (-1.0 / 256.0))
 
 
-def kernel(n, rl_ref, x_ref, ql_ref, ls_ref, o_ref, xf, qb, wb, w_s, prod, part, own, s3, r1, r3,
+def kernel(n, rl_ref, x_ref, ql_ref, ls_ref, o_ref, xf, qb, wb, w_s, prod, part, own, s3, r1, r3, grid, turn,
            ss1, rs1, ss3, rs3):
     trees, rows = rl_ref.shape
     width = x_ref.shape[0]
@@ -35,7 +40,8 @@
     t = queries // n
     nz = n // 2
     sub = nz * t
-    cols = width * width // CHUNKS
+    per_chunk = len(blocks_of(width)) // CHUNKS
+    cols = per_chunk * SIDE * SIDE
     me = lax.axis_index("rows")
     core = lax.rem(me, 2)
     z = me // 2
@@ -91,22 +97,21 @@
 
     lax.fori_loop(0, (rows // (halves * LANES)) * (queries // tile), weights_step, 0)
 
-    per_chunk = width // CHUNKS // GROUP
+    blocks = blocks_of(width)
+    area = SIDE * SIDE
 
     def compute(c):
-        def body(g, carry):
-            for jj in range(GROUP):
-                j = (c * per_chunk + g) * GROUP + jj
-                xb = jnp.broadcast_to(xf[pl.ds(j, 1), :], (16, rows)).astype(jnp.bfloat16)
-                for k in range(0, width, 16):
-                    prod[jj * width + k:jj * width + k + 16, :] = x_ref[k:k + 16, :] * xb
-            res = lax.dot_general(w_s[...], prod[...], (((1,), (1,)), ((), ())),
+        for g in range(per_chunk):
+            first, second = blocks[c * per_chunk + g]
+            right = x_ref[second * SIDE:(second + 1) * SIDE, :]
+            for jj in range(SIDE):
+                j = first * SIDE + jj
+                xb = jnp.broadcast_to(xf[j:j + 1, :], (SIDE, rows)).astype(jnp.bfloat16)
+                prod[g % 2, jj * SIDE:(jj + 1) * SIDE, :] = right * xb
+            res = lax.dot_general(w_s[...], prod[g % 2], (((1,), (1,)), ((), ())),
                                   preferred_element_type=jnp.float32)
-            off = pl.multiple_of(g * GROUP * width, GROUP * width)
             for a in range(2):
-                part[c, a, :, pl.ds(off, GROUP * width)] = res[a * sub:(a + 1) * sub, :]
-            return carry
-        lax.fori_loop(0, per_chunk, body, 0)
+                part[c, a, :, g * area:(g + 1) * area] = res[a * sub:(a + 1) * sub, :]
 
     def copy(src, dst, ssem, rsem, peer):
         return pltpu.make_async_remote_copy(src_ref=src, dst_ref=dst, send_sem=ssem, recv_sem=rsem,
@@ -128,12 +133,48 @@
         for d in range(1, nz):
             c3(c, d).start()
 
+    count = width // SIDE
+
     def finish(c):
         total = own[c, z]
         for d in range(1, nz):
             c3(c, d).wait_recv()
             total = total + decoded(r3[c, d - 1])
-        o_ref[:, c * cols:(c + 1) * cols] = total
+        for g in range(per_chunk):
+            a, b = blocks[c * per_chunk + g]
+            block = total[:, g * area:(g + 1) * area]
+            grid[b, a * t:(a + 1) * t, :] = block
+            if a != b:
+                at = upper.index((a, b)) * t
+                turn[at:at + t, :] = block
+
+    upper = [(a, b) for a, b in blocks if a != b]
+
+    def mirror():
+        value = turn[...]
+        source = lax.broadcasted_iota(jnp.int32, (area, area), 0)
+        target = lax.broadcasted_iota(jnp.int32, (area, area), 1)
+        swap = jnp.where(source == lax.rem(target, SIDE) * SIDE + target // SIDE, 1.0, 0.0).astype(jnp.bfloat16)
+        turned = jnp.zeros(value.shape, jnp.float32)
+        for _ in range(3):
+            piece = value.astype(jnp.bfloat16)
+            turned = turned + jnp.dot(piece, swap, preferred_element_type=jnp.float32)
+            value = value - piece.astype(jnp.float32)
+        for i, (a, b) in enumerate(upper):
+            grid[a, b * t:(b + 1) * t, :] = turned[i * t:(i + 1) * t, :]
+        lane = lax.broadcasted_iota(jnp.int32, (count * t, LANES), 1)
+        group = lax.rem(lane, width) // SIDE
+        for tile_at in range(SIDE * width // LANES):
+            per_tile = LANES // width
+            src = tile_at * per_tile * SIDE
+            pick = src % LANES + lane // width * SIDE + lax.rem(lane, SIDE)
+            base = src // LANES * LANES
+            out = jnp.zeros((count * t, LANES), jnp.float32)
+            for b in range(count):
+                out = jnp.where(group == b, jnp.take_along_axis(grid[b, :, base:base + LANES], pick, axis=1), out)
+            for a in range(count):
+                at = a * SIDE * width + tile_at * LANES
+                o_ref[:, at:at + LANES] = out[a * t:(a + 1) * t, :]
 
     for c in range(CHUNKS):
         compute(c)
@@ -148,6 +189,7 @@
     exchange(CHUNKS - 1)
     for c in range(CHUNKS):
         finish(c)
+    mirror()
     for c in range(CHUNKS):
         c1(c).wait_send()
         for d in range(1, nz):
@@ -162,7 +204,9 @@
     t = queries // n
     nz = n // 2
     sub = nz * t
-    cols = width * width // CHUNKS
+    per_chunk = len(blocks_of(width)) // CHUNKS
+    cols = per_chunk * SIDE * SIDE
+    count = width // SIDE
     vmem = pl.BlockSpec(memory_space=pltpu.VMEM)
     f32 = jnp.float32
     dma = pltpu.SemaphoreType.DMA
@@ -176,12 +220,14 @@
             pltpu.VMEM((trees, queries, LANES), jnp.int32),
             pltpu.VMEM((trees, queries, LANES), f32),
             pltpu.VMEM((queries, rows), jnp.bfloat16),
-            pltpu.VMEM((GROUP * width, rows), jnp.bfloat16),
+            pltpu.VMEM((2, SIDE * SIDE, rows), jnp.bfloat16),
             pltpu.VMEM((CHUNKS, 2, sub, cols), f32),
             pltpu.VMEM((CHUNKS, nz, t, cols), f32),
             pltpu.VMEM((CHUNKS, nz, t, cols + LANES), jnp.int16),
             pltpu.VMEM((CHUNKS, sub, cols), f32),
             pltpu.VMEM((CHUNKS, nz - 1, t, cols + LANES), jnp.int16),
+            pltpu.VMEM((count, count * t, SIDE * SIDE), f32),
+            pltpu.VMEM((count * (count - 1) // 2 * t, SIDE * SIDE), f32),
             dma((CHUNKS,)), dma((CHUNKS,)),
             dma((CHUNKS, nz - 1)), dma((CHUNKS, nz - 1)),
         ],

time: 24.8 us -> 21 us (0.85)
  Pallas kernels: 23.1 us -> 19.3 us
    pallas_call x1, Pallas kernels: 23.1 us -> 19.3 us  [per_device(): pl.pallas_call(functools.partial(kernel, n), out_shape=jax.ShapeDtypeStru...]
where the time goes in v3:
time: 21 us; the launch traced here: 20.8 us
  Pallas kernels  19.3 us (92%)
  local copies, waits for them, and re-layouts  1.47 us (7%)
    pallas_call x1, Pallas kernels, per_device(): pl.pallas_call(functools.partial(kernel, n), out_shape=jax.ShapeDtypeStru...  19.3 us
    unnamed x1, local copies, waits for them, and re-layouts  1.47 us

profile of v3, /device:TPU:0, one launch (start us, length us, event | category | flops | bytes accessed | tf_op | source)
XLA Modules:
  0.0 20.8 jit_solution(13616474549646148229)
XLA Ops:
  0.0 19.3 %shard_map.46 = f32[4,4096]{1,0:T(4,128)} custom-call(s32[32,2048]{1,0:T(8,128)} %rl_ref.1, bf16[64,2048]{1,0:T(8,128)(2,1)} %x_ref.1, s32[32,64]{1,0:T(8,128)} %ql_ref.1, s32[32,128]{1,0:T(8,128)} %ls_ref.1), custom_call_target="tpu_custom_call" | custom-call | tf_op jit(solution)/shard_map/pallas_call | solution.py:213
  19.3 1.5 %copy.6 = f32[4,4096]{1,0:T(4,128)} copy(f32[4,4096]{1,0:T(4,128)} %shard_map.46) | data formatting | bytes 131072

commit v4 on v3

--- a/solution.py
+++ b/solution.py
@@ -7,9 +7,8 @@
 from jax.experimental.pallas import tpu as pltpu
 from jax.sharding import PartitionSpec as P
 
-CHUNKS = 2
+CHUNKS = 1
 SIDE = 16
-EARLY = 1
 LANES = 128
 
 
@@ -178,15 +177,11 @@
 
     for c in range(CHUNKS):
         compute(c)
-        if c == EARLY - 1:
-            pl.semaphore_wait(barrier, nz)
-            for e in range(EARLY):
-                c1(e).start()
-        if c >= EARLY:
-            c1(c).start()
-            for e in (range(EARLY) if c == EARLY else [c - 1]):
-                exchange(e)
-    exchange(CHUNKS - 1)
+    pl.semaphore_wait(barrier, nz)
+    for c in range(CHUNKS):
+        c1(c).start()
+    for c in range(CHUNKS):
+        exchange(c)
     for c in range(CHUNKS):
         finish(c)
     mirror()

time: 21 us -> 20 us (0.952)
  Pallas kernels: 19.3 us -> 18.4 us
    pallas_call x1, Pallas kernels: 19.3 us -> 18.4 us  [per_device(): pl.pallas_call(functools.partial(kernel, n), out_shape=jax.ShapeDtypeStru...]
where the time goes in v4:
time: 20 us; the launch traced here: 19.8 us
  Pallas kernels  18.4 us (92%)
  local copies, waits for them, and re-layouts  1.47 us (7%)
    pallas_call x1, Pallas kernels, per_device(): pl.pallas_call(functools.partial(kernel, n), out_shape=jax.ShapeDtypeStru...  18.4 us
    unnamed x1, local copies, waits for them, and re-layouts  1.47 us

profile of v4, /device:TPU:0, one launch (start us, length us, event | category | flops | bytes accessed | tf_op | source)
XLA Modules:
  0.0 19.8 jit_solution(12564864633346724346)
XLA Ops:
  0.0 18.4 %shard_map.46 = f32[4,4096]{1,0:T(4,128)} custom-call(s32[32,2048]{1,0:T(8,128)} %rl_ref.1, bf16[64,2048]{1,0:T(8,128)(2,1)} %x_ref.1, s32[32,64]{1,0:T(8,128)} %ql_ref.1, s32[32,128]{1,0:T(8,128)} %ls_ref.1), custom_call_target="tpu_custom_call" | custom-call | tf_op jit(solution)/shard_map/pallas_call | solution.py:208
  18.4 1.5 %copy.6 = f32[4,4096]{1,0:T(4,128)} copy(f32[4,4096]{1,0:T(4,128)} %shard_map.46) | data formatting | bytes 131072

commit v5 on v4

--- a/solution.py
+++ b/solution.py
@@ -129,7 +129,7 @@
         for k in range(nz):
             own[c, k] = total[k * t:(k + 1) * t, :]
             s3[c, k] = code[k * t:(k + 1) * t, :].astype(jnp.int16)
-        for d in range(1, nz):
+        for d in sorted(range(1, nz), key=lambda d: abs(d - nz // 2)):
             c3(c, d).start()
 
     count = width // SIDE

time: 20 us -> 22.2 us (1.11)
  Pallas kernels: 18.4 us -> 20.6 us
    pallas_call x1, Pallas kernels: 18.4 us -> 20.6 us  [per_device(): pl.pallas_call(functools.partial(kernel, n), out_shape=jax.ShapeDtypeStru...]
where the time goes in v5:
time: 22.2 us; the launch traced here: 22 us
  Pallas kernels  20.6 us (93%)
  local copies, waits for them, and re-layouts  1.47 us (7%)
    pallas_call x1, Pallas kernels, per_device(): pl.pallas_call(functools.partial(kernel, n), out_shape=jax.ShapeDtypeStru...  20.6 us
    unnamed x1, local copies, waits for them, and re-layouts  1.47 us

profile of v5, /device:TPU:0, one launch (start us, length us, event | category | flops | bytes accessed | tf_op | source)
XLA Modules:
  0.0 22.0 jit_solution(240625525268436549)
XLA Ops:
  0.0 20.6 %shard_map.46 = f32[4,4096]{1,0:T(4,128)} custom-call(s32[32,2048]{1,0:T(8,128)} %rl_ref.1, bf16[64,2048]{1,0:T(8,128)(2,1)} %x_ref.1, s32[32,64]{1,0:T(8,128)} %ql_ref.1, s32[32,128]{1,0:T(8,128)} %ls_ref.1), custom_call_target="tpu_custom_call" | custom-call | tf_op jit(solution)/shard_map/pallas_call | solution.py:208
  20.6 1.5 %copy.6 = f32[4,4096]{1,0:T(4,128)} copy(f32[4,4096]{1,0:T(4,128)} %shard_map.46) | data formatting | bytes 131072
